TPU v7x, 32 devices: a whole 2x2x4 slice. The times are simulated.
32 devices in a mesh: wide: 8 (over y, x, core), samp: 4 (over z).
Axes of the slice: x: 2, y: 2, z: 4, core: 2. Of those that a mesh axis runs over, the one named last changes fastest.
Arguments:
- features: bfloat16 [4, 32, 96, 128], P('samp', 'wide'), may hold values from -6 to 6
- labels: int32 [4, 32, 96], P('samp', 'wide'), may hold values from 0 to 8
- conv_weight: bfloat16 [3, 3, 128, 128], replicated, may hold values from -0.1875 to 0.1875
- down_weight: bfloat16 [512, 1024], replicated, may hold values from -0.25 to 0.25
- expand_weight: bfloat16 [3, 3, 1024, 2048], P(None, None, None, 'wide'), may hold values from -0.0625 to 0.0625
- reduce_weight: bfloat16 [3, 3, 2048, 1024], P(None, None, 'wide'), may hold values from -0.046875 to 0.046875
- up_weight: bfloat16 [1024, 512], replicated, may hold values from -0.1875 to 0.1875
- class_weight: bfloat16 [128, 9], replicated, may hold values from -3 to 3
Outputs:
- conv_grad: float32 [3, 3, 128, 128], replicated
- down_grad: float32 [512, 1024], replicated
- expand_grad: float32 [3, 3, 1024, 2048], P(None, None, 'samp', 'wide')
- reduce_grad: float32 [3, 3, 2048, 1024], P(None, None, 'wide', 'samp')
- up_grad: float32 [1024, 512], replicated
- class_grad: float32 [128, 9], replicated
All inputs are finite; a program needn't handle non-finite values.
Results may differ from a plain program's by a relative error of at most 0.012.
Values may be sent and summed in bfloat16 or wider, within the bound.
No kernel may reach another device: no remote copies, remote signals or barrier semaphores. Data moves between devices by JAX's collectives and lax.ppermute only.
A program may use at most 192 MiB of HBM per device.

v0:
```python
import math
import jax
import jax.numpy as jnp
from jax import lax
from jax.sharding import PartitionSpec as P


def extended(block, sides, width):
    for axis, dim in sides:
        count = lax.axis_size(axis)
        forward = [(i, i + 1) for i in range(count - 1)]
        backward = [(target, source) for source, target in forward]
        low = lax.ppermute(
            lax.slice_in_dim(block, block.shape[dim] - width, None, axis=dim), axis, forward
        )
        high = lax.ppermute(lax.slice_in_dim(block, 0, width, axis=dim), axis, backward)
        block = jnp.concatenate([low, block, high], axis=dim)
    return block


def silu_slope(value):
    logistic = jax.nn.sigmoid(value)
    return logistic * (1.0 + value * (1.0 - logistic))


def pad_both(values):
    return jnp.pad(values, ((1, 1), (1, 1), (0, 0)))


def to_depth(grid):
    height, across, channels = grid.shape
    blocks = grid.reshape(height // 2, 2, across // 2, 2, channels)
    return jnp.transpose(blocks, (0, 2, 1, 3, 4)).reshape(height // 2, across // 2, 4 * channels)


def from_depth(grid):
    height, across, channels = grid.shape
    blocks = grid.reshape(height, across, 2, 2, channels // 4)
    return jnp.transpose(blocks, (0, 2, 1, 3, 4)).reshape(2 * height, 2 * across, channels // 4)


def taps_in(padded, height, across):
    return jnp.concatenate(
        [padded[p : p + height, q : q + across] for p in range(3) for q in range(3)], axis=-1
    )


def taps_out(values):
    return jnp.concatenate(
        [jnp.pad(values, ((p, 2 - p), (q, 2 - q), (0, 0))) for p in range(3) for q in range(3)],
        axis=-1,
    )


def conv_padded(padded, weight):
    height = padded.shape[0] - 2
    across = padded.shape[1] - 2
    inward = weight.shape[2]
    outward = weight.shape[3]
    if inward <= outward:
        window = taps_in(padded, height, across).reshape(height * across, 9 * inward)
        result = jnp.dot(
            window, weight.reshape(9 * inward, outward), preferred_element_type=jnp.float32
        )
        return result.reshape(height, across, outward)
    flattened = padded.reshape((height + 2) * (across + 2), inward)
    stacked = jnp.transpose(weight, (2, 0, 1, 3)).reshape(inward, 9 * outward)
    spread_out = jnp.dot(flattened, stacked, preferred_element_type=jnp.float32).reshape(
        height + 2, across + 2, 9, outward
    )
    summed = spread_out[0:height, 0:across, 0]
    for offset in range(1, 9):
        p = offset // 3
        q = offset % 3
        summed = summed + spread_out[p : p + height, q : q + across, offset]
    return summed


def correlate(padded, values):
    height, across, outward = values.shape
    inward = padded.shape[-1]
    if inward <= outward:
        window = taps_in(padded, height, across).reshape(height * across, 9 * inward)
        result = lax.dot_general(
            window,
            values.reshape(height * across, outward),
            (((0,), (0,)), ((), ())),
            preferred_element_type=jnp.float32,
        )
        return result.reshape(3, 3, inward, outward)
    shifted = taps_out(values).reshape((height + 2) * (across + 2), 9 * outward)
    result = lax.dot_general(
        padded.reshape(-1, inward),
        shifted,
        (((0,), (0,)), ((), ())),
        preferred_element_type=jnp.float32,
    )
    return jnp.transpose(result.reshape(inward, 3, 3, outward), (1, 2, 0, 3))


def contract_rows(left, right):
    left_flat = left.reshape(-1, left.shape[-1])
    right_flat = right.reshape(-1, right.shape[-1])
    return lax.dot_general(
        left_flat, right_flat, (((0,), (0,)), ((), ())), preferred_element_type=jnp.float32
    )


def flip_kernel(weight):
    return jnp.transpose(weight[::-1, ::-1], (0, 1, 3, 2))


def keep_rows(block_rows, first_row):
    return block_rows


def project_rows(values, weight):
    return jnp.dot(values, weight, preferred_element_type=jnp.float32).astype(jnp.bfloat16)


def widen_rows(values, weight):
    return lax.dot_general(
        values, weight, (((2,), (1,)), ((), ())), preferred_element_type=jnp.float32
    ).astype(jnp.bfloat16)


def collect(values, transform):
    return transform(lax.all_gather(values, "wide", axis=0, tiled=True), jnp.int32(0))


def spread_sum(term_rows, all_rows):
    whole_term = term_rows(0, all_rows)[None]
    pieces = lax.all_to_all(
        whole_term.astype(jnp.bfloat16), "wide", split_axis=1, concat_axis=0, tiled=True
    ).astype(whole_term.dtype)
    return jnp.sum(pieces, axis=0)


def local(
    features,
    labels,
    conv_weight,
    down_weight,
    expand_weight,
    reduce_weight,
    up_weight,
    class_weight,
):
    crop_rows = features[0]
    label_map = labels[0]
    height, across, channels = crop_rows.shape
    pixel_count = lax.axis_size("wide") * lax.axis_size("samp") * height * across
    loss_scale = 8.0 / math.sqrt(pixel_count)
    classes = lax.broadcasted_iota(jnp.int32, (1, 1, class_weight.shape[1]), 2)
    near_rows = extended(crop_rows, (("wide", 0),), 1)
    padded_in = jnp.pad(near_rows, ((0, 0), (1, 1), (0, 0)))
    hidden_pre = conv_padded(padded_in, conv_weight)
    hidden = jax.nn.silu(hidden_pre).astype(jnp.bfloat16)
    stacked = to_depth(hidden)
    coarse = project_rows(stacked, down_weight)
    coarse_all = collect(coarse, keep_rows)
    all_rows = coarse_all.shape[0]
    coarse_pad = pad_both(coarse_all)
    expand_pre = conv_padded(coarse_pad, expand_weight)
    expanded = jax.nn.silu(expand_pre).astype(jnp.bfloat16)
    expand_pad = pad_both(expanded)

    def reduce_block(first_row, row_count):
        return conv_padded(expand_pad, reduce_weight)

    bottom = (coarse.astype(jnp.float32) + spread_sum(reduce_block, all_rows)).astype(jnp.bfloat16)
    upward = from_depth(jnp.dot(bottom, up_weight, preferred_element_type=jnp.float32))
    joined_pre = upward + hidden.astype(jnp.float32)
    joined = jax.nn.silu(joined_pre).astype(jnp.bfloat16)
    logits = jnp.dot(joined, class_weight, preferred_element_type=jnp.float32)
    exp_logits = jnp.exp(logits)
    probability = exp_logits / jnp.sum(exp_logits, axis=-1, keepdims=True)
    onehot = (label_map[:, :, None] == classes).astype(jnp.float32)
    logit_grad = ((probability - onehot) * loss_scale).astype(jnp.bfloat16)
    class_grad = contract_rows(joined, logit_grad)
    joined_grad = lax.dot_general(
        logit_grad, class_weight, (((2,), (1,)), ((), ())), preferred_element_type=jnp.float32
    )
    upward_grad = (joined_grad * silu_slope(joined_pre)).astype(jnp.bfloat16)
    stacked_grad = to_depth(upward_grad)
    up_grad = contract_rows(bottom, stacked_grad)
    bottom_grad = widen_rows(stacked_grad, up_weight)
    bottom_all = collect(bottom_grad, keep_rows)
    reduce_grad = correlate(expand_pad, bottom_all)
    expanded_back = conv_padded(pad_both(bottom_all), flip_kernel(reduce_weight))
    expanded_grad = (expanded_back * silu_slope(expand_pre)).astype(jnp.bfloat16)
    expand_grad = correlate(coarse_pad, expanded_grad)
    grad_pad = pad_both(expanded_grad)
    back_expand = flip_kernel(expand_weight)

    def expand_back_block(first_row, row_count):
        return conv_padded(grad_pad, back_expand)

    coarse_grad = (
        bottom_grad.astype(jnp.float32) + spread_sum(expand_back_block, all_rows)
    ).astype(jnp.bfloat16)
    down_grad = contract_rows(stacked, coarse_grad)
    down_back = lax.dot_general(
        coarse_grad, down_weight, (((2,), (1,)), ((), ())), preferred_element_type=jnp.float32
    )
    hidden_sum = from_depth(down_back) + upward_grad.astype(jnp.float32)
    hidden_grad = (hidden_sum * silu_slope(hidden_pre)).astype(jnp.bfloat16)
    conv_grad = correlate(padded_in, hidden_grad)
    conv_grad, down_grad, up_grad, class_grad = lax.psum(
        (conv_grad, down_grad, up_grad, class_grad), ("wide", "samp")
    )
    expand_grad, reduce_grad = (
        lax.psum_scatter(
            expand_grad.astype(jnp.bfloat16), "samp", scatter_dimension=2, tiled=True
        ).astype(jnp.float32),
        lax.psum_scatter(
            reduce_grad.astype(jnp.bfloat16), "samp", scatter_dimension=3, tiled=True
        ).astype(jnp.float32),
    )
    return (conv_grad, down_grad, expand_grad, reduce_grad, up_grad, class_grad)


def solution(mesh):
    return jax.shard_map(
        local,
        mesh=mesh,
        in_specs=(
            P("samp", "wide", None, None),
            P("samp", "wide", None),
            P(),
            P(),
            P(None, None, None, "wide"),
            P(None, None, "wide", None),
            P(),
            P(),
        ),
        out_specs=(
            P(),
            P(),
            P(None, None, "samp", "wide"),
            P(None, None, "wide", "samp"),
            P(),
            P(),
        ),
        check_vma=False,
    )
```

profile of v0, /device:TPU:0, one launch (start us, length us, event | category | flops | bytes accessed | tf_op | source)
XLA Modules:
  0.0 500.4 jit_solution(18291208784481795078)
XLA Ops:
  8.1 2.4 collective-permute-start
  11.8 3.9 collective-permute-done.1
  21.6 2.0 multiply_convert_fusion.3
  24.9 6.7 %copy.50 = bf16[3,3,1024,256]{2,3,1,0:T(8,128)(2,1)} copy(bf16[3,3,1024,256]{3,2,1,0:T(8,128)(2,1)} %param.12) | data formatting | bytes 9437184 | tf_op args[4]
  31.5 22.4 %all-gather.3.cloned.1.call-done = bf16[16,48,1024]{2,1,0:T(8,128)(2,1)} async-done(((bf16[2,48,1024]{2,1,0:T(8,128)(2,1)}), bf16[16,48,1024]{2,1,0:T(8,128)(2,1)}) %all-gather.3.cloned.1.call-update) | async-done | bytes 1572880 | tf_op jit(solution)/shard_map/all_gather | solution.py:128
  54.0 8.0 %fusion.1 = f32[18,50,9,256]{3,1,2,0:T(8,128)S(1)} fusion(bf16[9,256,1024,1]{2,1,0,3:T(8,128)(2,1)} %bitcast.158, bf16[16,48,1024]{2,1,0:T(8,128)(2,1)} %all-gather.3.cloned.1.call-done), kind=kOutput, calls=%fused_computation.5 | convolution fusion | flops 4246732800 | bytes 14585856 | tf_op jit(solution)/shard_map/dot_general | solution.py:68
  64.4 3.8 fusion.7
  68.3 23.6 %all_to_all.8 = bf16[1,16,48,1024]{3,2,0,1:T(8,128)(2,1)S(1)} all-to-all(bf16[1,16,48,1024]{3,2,0,1:T(8,128)(2,1)S(1)} %fusion.7), channel_id=1, replica_groups=mesh['wide'=8,'samp'=4] {'wide'}, dimensions={1} | all-to-all | bytes 3145728 | tf_op jit(solution)/shard_map/all_to_all | solution.py:133
  96.0 4.9 rev.6
  100.9 2.1 pad.52
  103.0 1.7 reshape.178
  104.7 15.8 %all-gather.5.cloned.1.call-done = bf16[16,48,1024]{2,1,0:T(8,128)(2,1)} async-done(((bf16[2,48,1024]{2,1,0:T(8,128)(2,1)}), bf16[16,48,1024]{2,1,0:T(8,128)(2,1)}) %all-gather.5.cloned.1.call-update) | async-done | bytes 1572880 | tf_op jit(solution)/shard_map/all_gather | solution.py:128
  120.5 7.9 %fusion.3 = f32[18,50,9,256]{3,1,0,2:T(8,128)S(1)} fusion(bf16[9,256,1024,1]{2,1,3,0:T(8,128)(2,1)} %bitcast.165, bf16[16,48,1024]{2,1,0:T(8,128)(2,1)} %all-gather.5.cloned.1.call-done), kind=kOutput, calls=%fused_computation.7 | convolution fusion | flops 4246732800 | bytes 14585856 | tf_op jit(solution)/shard_map/dot_general | solution.py:68
  137.9 6.0 %reshape.153 = bf16[900,2304]{1,0:T(8,128)(2,1)} reshape(bf16[18,50,2304]{2,1,0:T(8,128)(2,1)} %pad_dynamic-update-slice_fusion.1) | data formatting | bytes 8294400 | tf_op jit(solution)/shard_map/reshape | solution.py:91
  143.9 6.6 %copy.66 = bf16[900,2304]{0,1:T(8,128)(2,1)} copy(bf16[900,2304]{1,0:T(8,128)(2,1)} %reshape.153) | data formatting | bytes 8294400 | tf_op jit(solution)/shard_map/reshape | solution.py:91
  150.5 9.3 %convert_bitcast_fusion = bf16[3,3,1024,256]{3,2,1,0:T(8,128)(2,1)} fusion(bf16[3,3,256,900]{3,2,1,0:T(8,128)(2,1)} %bitcast.166, bf16[900,1024,1,1]{1,0,2,3:T(8,128)(2,1)S(1)} %copy-done.9), kind=kOutput, calls=%fused_computation.1 | convolution fusion | flops 4249092096 | bytes 10708992 | tf_op jit(solution)/shard_map/dot_general | solution.py:92
  160.1 5.9 %copy.68 = bf16[2304,768]{1,0:T(8,128)(2,1)} copy(bf16[2304,768]{0,1:T(8,128)(2,1)} %bitcast.167) | data formatting | bytes 7077888 | tf_op jit(solution)/shard_map/dot_general | solution.py:84
  166.0 7.9 %convolution_convert_fusion = bf16[3,3,256,1024]{3,2,1,0:T(8,128)(2,1)} fusion(bf16[3,3,256,768]{3,2,1,0:T(8,128)(2,1)} %bitcast.168, bf16[768,1024,1,1]{1,0,3,2:T(8,128)(2,1)S(1)} %bitcast.195), kind=kOutput, calls=%fused_computation.4 | convolution fusion | flops 3626237952 | bytes 9830400 | tf_op jit(solution)/shard_map/dot_general | solution.py:84
  173.9 5.0 %rev.7 = bf16[3,3,1024,256]{2,3,1,0:T(8,128)(2,1)} reverse(bf16[3,3,1024,256]{2,3,1,0:T(8,128)(2,1)} %copy.50), dimensions={0,1} | reverse | bytes 9437184 | tf_op jit(solution)/shard_map/rev | solution.py:110
  181.2 4.9 fusion.8
  186.1 3.7 all-to-all-start.1
  191.9 1.8 copy.48
  195.3 2.8 fusion.64
  198.1 12.8 %all-to-all-done.1 = bf16[1,16,48,1024]{3,2,0,1:T(8,128)(2,1)S(1)} async-done(((bf16[1,16,48,1024]{3,2,0,1:T(8,128)(2,1)}), bf16[1,16,48,1024]{3,2,0,1:T(8,128)(2,1)S(1)}, u32[]{:S(2)}, u32[]{:S(2)}) %all-to-all-start.1) | async-done | bytes 1572896 | tf_op jit(solution)/shard_map/all_to_all | solution.py:133
  215.1 1.8 fusion.63
  217.1 42.5 %psum.31 = f32[128,9]{0,1:T(8,128)} all-reduce(f32[128,9]{0,1:T(8,128)S(1)} %convolution_bitcast_fusion), channel_id=1, replica_groups=mesh['wide'=8,'samp'=4] {'wide','samp'}, use_global_device_ids=true, to_apply=%region_8.9 | all-reduce | flops 1152 | bytes 9216 | tf_op jit(solution)/shard_map/psum | solution.py:209
  259.6 2.9 convert_element_type.144
  262.5 71.5 %reduce-scatter.5.cloned.1.call-done = bf16[3,3,256,256]{3,2,1,0:T(8,128)(2,1)} async-done(((bf16[3,3,256,1024]{3,2,1,0:T(8,128)(2,1)}), bf16[3,3,256,256]{3,2,1,0:T(8,128)(2,1)}) %reduce-scatter.5.cloned.1.call-update) | async-done | bytes 1179664 | tf_op jit(solution)/shard_map/reduce_scatter | solution.py:216
  334.0 2.9 convert_element_type.146
  336.9 150.4 %all-reduce.16.cloned.1.call-done = (f32[3,3,128,128]{3,2,1,0:T(8,128)}, f32[512,1024]{1,0:T(8,128)}, f32[1024,512]{1,0:T(8,128)}) async-done(((f32[3,3,128,128]{3,2,1,0:T(8,128)}, f32[512,1024]{1,0:T(8,128)}, f32[1024,512]{1,0:T(8,128)}), (f32[3,3,128,128]{3,2,1,0:T(8,128)}, f32[512,1024]{1,0:T(8,128)}, f32[1024,512]{1,0:T(8,128)})) %all-reduce.16.cloned.1.call-update) | async-done | bytes 4784144 | tf_op jit(solution)/shard_map/psum | solution.py:209
  487.3 2.1 copy.123
  489.4 3.2 copy.124
  (144 shorter events, 36.9 us)
Async XLA Ops:
  7.2 85.8 %copy-start = (bf16[1024,512]{1,0:T(8,128)(2,1)S(1)}, bf16[1024,512]{1,0:T(8,128)(2,1)}, u32[]{:S(2)}) copy-start(bf16[1024,512]{1,0:T(8,128)(2,1)} %param.14) | copy-start | bytes 3145732
  7.2 16.6 %copy-start.4 = (bf16[512,1024]{1,0:T(8,128)(2,1)S(1)}, bf16[512,1024]{1,0:T(8,128)(2,1)}, u32[]{:S(2)}) copy-start(bf16[512,1024]{1,0:T(8,128)(2,1)} %param.11) | copy-start | bytes 3145732
  7.2 46.8 %all-gather.3.cloned.1.call-start = ((), (), s32[]{:S(2)}) async-start(), calls=%async_computation.4 | async-start | bytes 1769472 | tf_op jit(solution)/shard_map/all_gather | solution.py:128
  8.1 3.7 collective-permute-start
  10.5 5.2 %collective-permute-start.1 = (bf16[1,96,128]{2,1,0:T(8,128)(2,1)S(1)}, bf16[1,96,128]{2,1,0:T(8,128)(2,1)S(1)}, u32[]{:S(2)}, u32[]{:S(2)}) collective-permute-start(bf16[1,96,128]{2,1,0:T(8,128)(2,1)S(1)} %get-tuple-element.23), channel_id=1, source_target_pairs={{4,0},{8,4},{12,8},{16,12},{20,16},{24,20},{28,24},{5,1},{9,5},{13... | collective-permute-start | bytes 73736 | tf_op jit(solution)/shard_map/ppermute | solution.py:16
  24.8 95.7 %all-gather.5.cloned.1.call-start = ((), (), s32[]{:S(2)}) async-start(), calls=%async_computation.5 | async-start | bytes 1769472 | tf_op jit(solution)/shard_map/all_gather | solution.py:128
  54.0 10.4 %slice-start = ((s8[4718592]{0:T(1024)(128)(4,1)}), s8[4194304]{0:T(1024)(128)(4,1)S(1)}, s32[]{:S(2)}) async-start(s8[4718592]{0:T(1024)(128)(4,1)} %bitcast.161), calls=%async_computation.9 | async-start | bytes 8388608
  54.0 10.4 %slice-start.1 = ((s8[4718592]{0:T(1024)(128)(4,1)}), s8[524288]{0:T(1024)(128)(4,1)S(1)}, s32[]{:S(2)}) async-start(s8[4718592]{0:T(1024)(128)(4,1)} %bitcast.161), calls=%async_computation.10 | async-start | bytes 1048576
  64.4 3.9 copy-start.3
  68.3 23.9 %copy-start.11 = (bf16[2,48,1024]{2,1,0:T(8,128)(2,1)S(1)}, bf16[2,48,1024]{2,1,0:T(8,128)(2,1)}, u32[]{:S(2)}) copy-start(bf16[2,48,1024]{2,1,0:T(8,128)(2,1)} %convolution_convert_fusion.4) | copy-start | bytes 589828
  68.3 25.3 %copy-start.23 = (bf16[128,9]{0,1:T(8,128)(2,1)S(1)}, bf16[128,9]{0,1:T(8,128)(2,1)}, u32[]{:S(2)}) copy-start(bf16[128,9]{0,1:T(8,128)(2,1)} %param.15) | copy-start | bytes 6916
  91.9 2.3 copy-start.25
  94.4 1.5 copy-start.18
  95.7 163.9 %reduce-scatter.3.cloned.1.call-start = ((), (), s32[]{:S(2)}) async-start(), calls=%async_computation.6 | async-start | bytes 5898240 | tf_op jit(solution)/shard_map/reduce_scatter | solution.py:213
  120.5 7.9 %copy-start.6 = (f32[16,48,256]{2,1,0:T(8,128)S(1)}, f32[16,48,256]{2,1,0:T(8,128)}, u32[]{:S(2)}) copy-start(f32[16,48,256]{2,1,0:T(8,128)} %get-tuple-element.10) | copy-start | bytes 2359300
  143.9 6.6 %copy-start.9 = (bf16[900,1024,1,1]{1,0,2,3:T(8,128)(2,1)S(1)}, bf16[900,1024,1,1]{1,0,2,3:T(8,128)(2,1)}, u32[]{:S(2)}) copy-start(bf16[900,1024,1,1]{1,0,2,3:T(8,128)(2,1)} %reshape.178) | copy-start | bytes 5529604
  159.8 174.2 %reduce-scatter.5.cloned.1.call-start = ((), (), s32[]{:S(2)}) async-start(), calls=%async_computation.7 | async-start | bytes 5898240 | tf_op jit(solution)/shard_map/reduce_scatter | solution.py:216
  160.1 5.9 %copy-start.24 = (bf16[16,48,1024]{2,1,0:T(8,128)(2,1)S(1)}, bf16[16,48,1024]{2,1,0:T(8,128)(2,1)}, u32[]{:S(2)}) copy-start(bf16[16,48,1024]{2,1,0:T(8,128)(2,1)} %all-gather.5.cloned.1.call-done) | copy-start | bytes 4718596
  178.9 2.3 copy-start.2
  181.2 9.4 %copy-start.17 = (bf16[4,96,128]{2,1,0:T(8,128)(2,1)S(1)}, bf16[4,96,128]{2,1,0:T(8,128)(2,1)}, u32[]{:S(2)}) copy-start(bf16[4,96,128]{2,1,0:T(8,128)(2,1)} %get-tuple-element.20) | copy-start | bytes 294916
  186.1 4.5 copy-start.20
  186.1 4.6 copy-start.16
  186.1 4.6 copy-start.15
  186.1 4.7 copy-start.7
  186.1 4.8 copy-start.19
  186.1 24.7 %all-to-all-start.1 = ((bf16[1,16,48,1024]{3,2,0,1:T(8,128)(2,1)}), bf16[1,16,48,1024]{3,2,0,1:T(8,128)(2,1)S(1)}, u32[]{:S(2)}, u32[]{:S(2)}) async-start(bf16[1,16,48,1024]{3,2,0,1:T(8,128)(2,1)} %fusion.8), calls=%async_computation.1 | async-start | bytes 3145728 | tf_op jit(solution)/shard_map/all_to_all | solution.py:133
  189.9 297.4 %all-reduce.16.cloned.1.call-start = ((), (), s32[]{:S(2)}) async-start(), calls=%async_computation.8 | async-start | bytes 9568256 | tf_op jit(solution)/shard_map/psum | solution.py:209
  191.9 20.3 %copy-start.5 = (bf16[512,1024]{1,0:T(8,128)(2,1)S(1)}, bf16[512,1024]{1,0:T(8,128)(2,1)}, u32[]{:S(2)}) copy-start(bf16[512,1024]{1,0:T(8,128)(2,1)} %param.11) | copy-start | bytes 3145732
  211.1 4.0 copy-start.14
  215.1 1.8 copy-start.22
  487.3 5.2 %copy-start.8 = (f32[1024,512]{1,0:T(8,128)S(1)}, f32[1024,512]{1,0:T(8,128)}, u32[]{:S(2)}) copy-start(f32[1024,512]{1,0:T(8,128)} %get-tuple-element.30) | copy-start | bytes 6291460
  487.3 6.6 %copy-start.1 = (bf16[1024,512]{1,0:T(8,128)(2,1)S(1)}, bf16[1024,512]{1,0:T(8,128)(2,1)}, u32[]{:S(2)}) copy-start(bf16[1024,512]{1,0:T(8,128)(2,1)} %param.14) | copy-start | bytes 3145732
  (4 other events, 3.7 us)
Sparse Core Ops, SparseCore 0:
  25.0 28.9 all-gather.2
  95.8 24.6 all-gather.4
  159.9 85.9 reduce-scatter.2
  248.1 85.8 reduce-scatter.4
  340.5 146.7 all-reduce.15
where the time goes:
time: 502 us; the launch traced here: 500 us
  waiting for transfers between devices  277 us (55%)
  local copies, waits for them, and re-layouts  66.8 us (13%)
  blocking collectives  66.1 us (13%)
  matrix products  53 us (11%)
  other arithmetic  15.1 us (3%)
  between operations  14.5 us (3%)
  starting transfers between devices  8.02 us (2%)
    psum x1, waiting for transfers between devices, local(): lax.psum((conv_grad, down_grad, up_grad, class_grad), ('wide', 'samp'))  150 us
    reduce_scatter x1, waiting for transfers between devices, local(): lax.psum_scatter(reduce_grad.astype(jnp.bfloat16), 'samp', scatter_dimens...  71.5 us
    psum x1, blocking collectives, local(): lax.psum((conv_grad, down_grad, up_grad, class_grad), ('wide', 'samp'))  42.5 us
    all_gather x2, waiting for transfers between devices, collect(): lax.all_gather(values, 'wide', axis=0, tiled=True)  38.2 us
    unnamed x98, local copies, waits for them, and re-layouts  27 us
    all_to_all x1, blocking collectives, spread_sum(): lax.all_to_all(whole_term.astype(jnp.bfloat16), 'wide', split_axis=1, con...  23.6 us
    dot_general x2, matrix products, conv_padded(): jnp.dot(flattened, stacked, preferred_element_type=jnp.float32)  15.9 us
    all_to_all x1, waiting for transfers between devices, spread_sum(): lax.all_to_all(whole_term.astype(jnp.bfloat16), 'wide', split_axis=1, con...  12.8 us
  transfers between devices with their start and end apart: 8, of which 6 were waited for; matrix products, arithmetic and copies ran while one was open for 12% of the time, Pallas kernels for 0%

commit v1 on v0

--- a/solution.py
+++ b/solution.py
@@ -207,7 +207,7 @@
     hidden_grad = (hidden_sum * silu_slope(hidden_pre)).astype(jnp.bfloat16)
     conv_grad = correlate(padded_in, hidden_grad)
     conv_grad, down_grad, up_grad, class_grad = lax.psum(
-        (conv_grad, down_grad, up_grad, class_grad), ("wide", "samp")
+        lax.psum((conv_grad, down_grad, up_grad, class_grad), "samp"), "wide"
     )
     expand_grad, reduce_grad = (
         lax.psum_scatter(

time: 502 us -> 618 us (1.23)
  waiting for transfers between devices: 277 us -> 419 us
  blocking collectives: 66.1 us -> 46.8 us
    psum x1 -> x2, waiting for transfers between devices: 150 us -> 214 us  [the longest x1 126 us: local(): lax.psum((conv_grad, down_grad, up_grad, class_grad), 'samp')]
    reduce_scatter x1, waiting for transfers between devices: 0.01 us -> 63.1 us  [local(): lax.psum_scatter(expand_grad.astype(jnp.bfloat16), 'samp', scatter_dimens...]
    psum x1 -> x2, blocking collectives: 42.5 us -> 23.2 us  [the longest x1 13.5 us: local(): lax.psum(lax.psum((conv_grad, down_grad, up_grad, class_grad), 'samp'), '...]
    reduce_scatter x1, waiting for transfers between devices: 71.5 us -> 85 us  [local(): lax.psum_scatter(reduce_grad.astype(jnp.bfloat16), 'samp', scatter_dimens...]
    unnamed x98 -> x94, local copies, waits for them, and re-layouts: 27 us -> 25.9 us
  transfers between devices with their start and end apart: 8 -> 9, of which waited for: 6 -> 8; matrix products, arithmetic and copies ran while one was open for 12% -> 12% of each run, Pallas kernels for 0% -> 0%
where the time goes in v1:
time: 618 us; the launch traced here: 617 us
  waiting for transfers between devices  419 us (68%)
  local copies, waits for them, and re-layouts  63.7 us (10%)
  matrix products  53.9 us (9%)
  blocking collectives  46.8 us (8%)
  between operations  14.8 us (2%)
  other arithmetic  11.1 us (2%)
  starting transfers between devices  7.86 us (1%)
    psum x1, waiting for transfers between devices, local(): lax.psum((conv_grad, down_grad, up_grad, class_grad), 'samp')  126 us
    psum x1, waiting for transfers between devices, local(): lax.psum(lax.psum((conv_grad, down_grad, up_grad, class_grad), 'samp'), '...  88.7 us
    reduce_scatter x1, waiting for transfers between devices, local(): lax.psum_scatter(reduce_grad.astype(jnp.bfloat16), 'samp', scatter_dimens...  85 us
    reduce_scatter x1, waiting for transfers between devices, local(): lax.psum_scatter(expand_grad.astype(jnp.bfloat16), 'samp', scatter_dimens...  63.1 us
    all_gather x2, waiting for transfers between devices, collect(): lax.all_gather(values, 'wide', axis=0, tiled=True)  37 us
    unnamed x94, local copies, waits for them, and re-layouts  25.9 us
    all_to_all x1, blocking collectives, spread_sum(): lax.all_to_all(whole_term.astype(jnp.bfloat16), 'wide', split_axis=1, con...  23.6 us
    dot_general x2, matrix products, conv_padded(): jnp.dot(flattened, stacked, preferred_element_type=jnp.float32)  15.8 us
  transfers between devices with their start and end apart: 9, of which 8 were waited for; matrix products, arithmetic and copies ran while one was open for 12% of the time, Pallas kernels for 0%

profile of v1, /device:TPU:0, one launch (start us, length us, event | category | flops | bytes accessed | tf_op | source)
XLA Modules:
  0.0 616.7 jit_solution(18036788994754916078)
XLA Ops:
  8.1 2.4 collective-permute-start
  11.8 3.9 collective-permute-done.1
  19.8 2.0 multiply_convert_fusion.3
  23.0 6.6 %copy.50 = bf16[3,3,1024,256]{2,3,1,0:T(8,128)(2,1)} copy(bf16[3,3,1024,256]{3,2,1,0:T(8,128)(2,1)} %param.12) | data formatting | bytes 9437184 | tf_op args[4]
  29.7 22.4 %all-gather.3.cloned.1.call-done = bf16[16,48,1024]{2,1,0:T(8,128)(2,1)} async-done(((bf16[2,48,1024]{2,1,0:T(8,128)(2,1)}), bf16[16,48,1024]{2,1,0:T(8,128)(2,1)}) %all-gather.3.cloned.1.call-update) | async-done | bytes 1572880 | tf_op jit(solution)/shard_map/all_gather | solution.py:128
  52.1 8.0 %fusion.1 = f32[18,50,9,256]{3,1,2,0:T(8,128)S(1)} fusion(bf16[9,256,1024,1]{2,1,0,3:T(8,128)(2,1)} %bitcast.158, bf16[16,48,1024]{2,1,0:T(8,128)(2,1)} %all-gather.3.cloned.1.call-done), kind=kOutput, calls=%fused_computation.5 | convolution fusion | flops 4246732800 | bytes 14585856 | tf_op jit(solution)/shard_map/dot_general | solution.py:68
  61.7 3.8 fusion.7
  65.5 23.6 %all_to_all.8 = bf16[1,16,48,1024]{3,2,0,1:T(8,128)(2,1)S(1)} all-to-all(bf16[1,16,48,1024]{3,2,0,1:T(8,128)(2,1)S(1)} %fusion.7), channel_id=1, replica_groups=mesh['wide'=8,'samp'=4] {'wide'}, dimensions={1} | all-to-all | bytes 3145728 | tf_op jit(solution)/shard_map/all_to_all | solution.py:133
  93.0 5.0 rev.6
  98.0 5.2 rev.7
  103.2 14.6 %all-gather.5.cloned.1.call-done = bf16[16,48,1024]{2,1,0:T(8,128)(2,1)} async-done(((bf16[2,48,1024]{2,1,0:T(8,128)(2,1)}), bf16[16,48,1024]{2,1,0:T(8,128)(2,1)}) %all-gather.5.cloned.1.call-update) | async-done | bytes 1572880 | tf_op jit(solution)/shard_map/all_gather | solution.py:128
  117.8 7.8 %fusion.3 = f32[18,50,9,256]{3,1,0,2:T(8,128)S(1)} fusion(bf16[9,256,1024,1]{2,1,3,0:T(8,128)(2,1)} %bitcast.167, bf16[16,48,1024]{2,1,0:T(8,128)(2,1)} %all-gather.5.cloned.1.call-done), kind=kOutput, calls=%fused_computation.7 | convolution fusion | flops 4246732800 | bytes 14585856 | tf_op jit(solution)/shard_map/dot_general | solution.py:68
  128.0 4.9 fusion.8
  132.8 3.7 all-to-all-start.1
  142.3 15.2 %all-to-all-done.1 = bf16[1,16,48,1024]{3,2,0,1:T(8,128)(2,1)S(1)} async-done(((bf16[1,16,48,1024]{3,2,0,1:T(8,128)(2,1)}), bf16[1,16,48,1024]{3,2,0,1:T(8,128)(2,1)S(1)}, u32[]{:S(2)}, u32[]{:S(2)}) %all-to-all-start.1) | async-done | bytes 1572896 | tf_op jit(solution)/shard_map/all_to_all | solution.py:133
  159.8 2.7 fusion.63
  163.9 2.1 pad.52
  176.1 6.0 reshape.153
  182.1 6.6 %copy.66 = bf16[900,2304]{0,1:T(8,128)(2,1)} copy(bf16[900,2304]{1,0:T(8,128)(2,1)} %reshape.153) | data formatting | bytes 8294400 | tf_op jit(solution)/shard_map/reshape | solution.py:91
  188.7 9.3 %convert_bitcast_fusion = bf16[3,3,1024,256]{3,2,1,0:T(8,128)(2,1)} fusion(bf16[3,3,256,900]{3,2,1,0:T(8,128)(2,1)} %bitcast.168, bf16[900,1024,1,1]{1,0,2,3:T(8,128)(2,1)S(1)} %copy-done.6), kind=kOutput, calls=%fused_computation.1 | convolution fusion | flops 4249092096 | bytes 10708992 | tf_op jit(solution)/shard_map/dot_general | solution.py:92
  198.1 5.9 copy.68
  204.0 7.6 %convolution_convert_fusion = bf16[3,3,256,1024]{3,2,1,0:T(8,128)(2,1)} fusion(bf16[3,3,256,768]{3,2,1,0:T(8,128)(2,1)} %bitcast.170, bf16[768,1024,1,1]{1,0,3,2:T(8,128)(2,1)S(1)} %bitcast.197), kind=kOutput, calls=%fused_computation.4 | convolution fusion | flops 3626237952 | bytes 9830400 | tf_op jit(solution)/shard_map/dot_general | solution.py:84
  211.7 125.5 %all-reduce.20.cloned.1.call-done = (f32[3,3,128,128]{3,2,1,0:T(8,128)}, f32[512,1024]{1,0:T(8,128)}, f32[1024,512]{1,0:T(8,128)}) async-done(((f32[3,3,128,128]{3,2,1,0:T(8,128)}, f32[512,1024]{1,0:T(8,128)}, f32[1024,512]{1,0:T(8,128)}), (f32[3,3,128,128]{3,2,1,0:T(8,128)}, f32[512,1024]{1,0:T(8,128)}, f32[1024,512]{1,0:T(8,128)})) %all-reduce.20.cloned.1.call-update) | async-done | bytes 4784144 | tf_op jit(solution)/shard_map/psum | solution.py:210
  337.4 9.7 %psum.62 = f32[128,9]{0,1:T(8,128)S(1)} all-reduce(f32[128,9]{0,1:T(8,128)S(1)} %convolution_bitcast_fusion), channel_id=1, replica_groups=mesh['wide'=8,'samp'=4] {'samp'}, use_global_device_ids=true, to_apply=%region_11.12 | all-reduce | flops 1152 | bytes 9216 | tf_op jit(solution)/shard_map/psum | solution.py:210
  347.1 13.5 %psum.63 = f32[128,9]{0,1:T(8,128)} all-reduce(f32[128,9]{0,1:T(8,128)S(1)} %psum.62), channel_id=1, replica_groups=mesh['wide'=8,'samp'=4] {'wide'}, use_global_device_ids=true, to_apply=%region_12.13 | all-reduce | flops 1152 | bytes 9216 | tf_op jit(solution)/shard_map/psum | solution.py:209
  360.6 63.1 %reduce-scatter.3.cloned.1.call-done = bf16[3,3,256,256]{3,2,1,0:T(8,128)(2,1)} async-done(((bf16[3,3,1024,256]{3,2,1,0:T(8,128)(2,1)}), bf16[3,3,256,256]{3,2,1,0:T(8,128)(2,1)}) %reduce-scatter.3.cloned.1.call-update) | async-done | bytes 1179664 | tf_op jit(solution)/shard_map/reduce_scatter | solution.py:213
  423.7 2.9 convert_element_type.144
  426.6 85.0 %reduce-scatter.5.cloned.1.call-done = bf16[3,3,256,256]{3,2,1,0:T(8,128)(2,1)} async-done(((bf16[3,3,256,1024]{3,2,1,0:T(8,128)(2,1)}), bf16[3,3,256,256]{3,2,1,0:T(8,128)(2,1)}) %reduce-scatter.5.cloned.1.call-update) | async-done | bytes 1179664 | tf_op jit(solution)/shard_map/reduce_scatter | solution.py:216
  511.6 2.9 convert_element_type.146
  514.5 88.7 %all-reduce.18.cloned.1.call-done = (f32[3,3,128,128]{3,2,1,0:T(8,128)}, f32[512,1024]{1,0:T(8,128)}, f32[1024,512]{1,0:T(8,128)}) async-done(((f32[3,3,128,128]{3,2,1,0:T(8,128)}, f32[512,1024]{1,0:T(8,128)}, f32[1024,512]{1,0:T(8,128)}), (f32[3,3,128,128]{3,2,1,0:T(8,128)}, f32[512,1024]{1,0:T(8,128)}, f32[1024,512]{1,0:T(8,128)})) %all-reduce.18.cloned.1.call-update) | async-done | bytes 4784144 | tf_op jit(solution)/shard_map/psum | solution.py:209
  603.3 2.1 copy.126
  605.3 3.2 copy.127
  (145 shorter events, 35.9 us)
Async XLA Ops:
  7.2 83.0 %copy-start = (bf16[1024,512]{1,0:T(8,128)(2,1)S(1)}, bf16[1024,512]{1,0:T(8,128)(2,1)}, u32[]{:S(2)}) copy-start(bf16[1024,512]{1,0:T(8,128)(2,1)} %param.14) | copy-start | bytes 3145732
  7.2 14.8 %copy-start.3 = (bf16[512,1024]{1,0:T(8,128)(2,1)S(1)}, bf16[512,1024]{1,0:T(8,128)(2,1)}, u32[]{:S(2)}) copy-start(bf16[512,1024]{1,0:T(8,128)(2,1)} %param.11) | copy-start | bytes 3145732
  7.2 44.9 %all-gather.3.cloned.1.call-start = ((), (), s32[]{:S(2)}) async-start(), calls=%async_computation.4 | async-start | bytes 1769472 | tf_op jit(solution)/shard_map/all_gather | solution.py:128
  8.1 3.7 collective-permute-start
  10.5 5.2 collective-permute-start.1
  23.0 94.8 %all-gather.5.cloned.1.call-start = ((), (), s32[]{:S(2)}) async-start(), calls=%async_computation.5 | async-start | bytes 1769472 | tf_op jit(solution)/shard_map/all_gather | solution.py:128
  52.1 9.6 %slice-start = ((s8[4718592]{0:T(1024)(128)(4,1)}), s8[4194304]{0:T(1024)(128)(4,1)S(1)}, s32[]{:S(2)}) async-start(s8[4718592]{0:T(1024)(128)(4,1)} %bitcast.161), calls=%async_computation.10 | async-start | bytes 8388608
  52.1 9.6 %slice-start.1 = ((s8[4718592]{0:T(1024)(128)(4,1)}), s8[524288]{0:T(1024)(128)(4,1)S(1)}, s32[]{:S(2)}) async-start(s8[4718592]{0:T(1024)(128)(4,1)} %bitcast.161), calls=%async_computation.11 | async-start | bytes 1048576
  61.6 3.9 copy-start.2
  65.5 23.9 %copy-start.10 = (bf16[2,48,1024]{2,1,0:T(8,128)(2,1)S(1)}, bf16[2,48,1024]{2,1,0:T(8,128)(2,1)}, u32[]{:S(2)}) copy-start(bf16[2,48,1024]{2,1,0:T(8,128)(2,1)} %convolution_convert_fusion.4) | copy-start | bytes 589828
  65.5 25.3 %copy-start.19 = (bf16[128,9]{0,1:T(8,128)(2,1)S(1)}, bf16[128,9]{0,1:T(8,128)(2,1)}, u32[]{:S(2)}) copy-start(bf16[128,9]{0,1:T(8,128)(2,1)} %param.15) | copy-start | bytes 6916
  89.2 2.3 copy-start.21
  91.7 6.3 %copy-start.14 = (bf16[4,96,128]{2,1,0:T(8,128)(2,1)}, bf16[4,96,128]{2,1,0:T(8,128)(2,1)S(1)}, u32[]{:S(2)}) copy-start(bf16[4,96,128]{2,1,0:T(8,128)(2,1)S(1)} %fusion.9) | copy-start | bytes 294916
  91.8 6.2 %copy-start.12 = (bf16[2,2,48,2,128]{4,3,1,2,0:T(2,128)(2,1)}, bf16[2,2,48,2,128]{4,3,1,2,0:T(2,128)(2,1)S(1)}, u32[]{:S(2)}) copy-start(bf16[2,2,48,2,128]{4,3,1,2,0:T(2,128)(2,1)S(1)} %copy.78) | copy-start | bytes 294916
  125.6 2.2 slice-start.2
  125.7 2.3 slice-start.3
  132.8 4.8 copy-start.4
  132.8 7.7 %copy-start.13 = (bf16[2,2,48,2,128]{4,3,1,2,0:T(2,128)(2,1)S(1)}, bf16[2,2,48,2,128]{4,3,1,2,0:T(2,128)(2,1)}, u32[]{:S(2)}) copy-start(bf16[2,2,48,2,128]{4,3,1,2,0:T(2,128)(2,1)} %copy-done.12) | copy-start | bytes 294916
  132.8 7.7 %copy-start.8 = (bf16[2,48,1024]{2,1,0:T(8,128)(2,1)S(1)}, bf16[2,48,1024]{2,1,0:T(8,128)(2,1)}, u32[]{:S(2)}) copy-start(bf16[2,48,1024]{2,1,0:T(8,128)(2,1)} %copy-done.7) | copy-start | bytes 589828
  132.8 24.7 %all-to-all-start.1 = ((bf16[1,16,48,1024]{3,2,0,1:T(8,128)(2,1)}), bf16[1,16,48,1024]{3,2,0,1:T(8,128)(2,1)S(1)}, u32[]{:S(2)}, u32[]{:S(2)}) async-start(bf16[1,16,48,1024]{3,2,0,1:T(8,128)(2,1)} %fusion.8), calls=%async_computation.1 | async-start | bytes 3145728 | tf_op jit(solution)/shard_map/all_to_all | solution.py:133
  136.6 200.6 %all-reduce.20.cloned.1.call-start = ((), (), s32[]{:S(2)}) async-start(), calls=%async_computation.9 | async-start | bytes 9568256 | tf_op jit(solution)/shard_map/psum | solution.py:210
  137.7 20.1 %copy-start.9 = (bf16[2,48,1024]{2,1,0:T(8,128)(2,1)S(1)}, bf16[2,48,1024]{2,1,0:T(8,128)(2,1)}, u32[]{:S(2)}) copy-start(bf16[2,48,1024]{2,1,0:T(8,128)(2,1)} %convolution_convert_fusion.3) | copy-start | bytes 589828
  157.8 4.7 copy-start.15
  157.8 4.7 copy-start.18
  163.8 259.9 %reduce-scatter.3.cloned.1.call-start = ((), (), s32[]{:S(2)}) async-start(), calls=%async_computation.6 | async-start | bytes 5898240 | tf_op jit(solution)/shard_map/reduce_scatter | solution.py:213
  182.1 6.6 %copy-start.6 = (bf16[900,1024,1,1]{1,0,2,3:T(8,128)(2,1)S(1)}, bf16[900,1024,1,1]{1,0,2,3:T(8,128)(2,1)}, u32[]{:S(2)}) copy-start(bf16[900,1024,1,1]{1,0,2,3:T(8,128)(2,1)} %reshape.178) | copy-start | bytes 5529604
  198.1 313.6 %reduce-scatter.5.cloned.1.call-start = ((), (), s32[]{:S(2)}) async-start(), calls=%async_computation.7 | async-start | bytes 5898240 | tf_op jit(solution)/shard_map/reduce_scatter | solution.py:216
  198.1 5.9 copy-start.20
  211.6 125.6 %copy-start.17 = (bf16[4,96,128]{2,1,0:T(8,128)(2,1)S(1)}, bf16[4,96,128]{2,1,0:T(8,128)(2,1)}, u32[]{:S(2)}) copy-start(bf16[4,96,128]{2,1,0:T(8,128)(2,1)} %copy-done.16) | copy-start | bytes 294916
  211.6 391.6 %all-reduce.18.cloned.1.call-start = ((), (), s32[]{:S(2)}) async-start(), calls=%async_computation.8 | async-start | bytes 9568256 | tf_op jit(solution)/shard_map/psum | solution.py:209
  603.3 5.2 copy-start.5
  603.3 6.6 %copy-start.1 = (bf16[1024,512]{1,0:T(8,128)(2,1)S(1)}, bf16[1024,512]{1,0:T(8,128)(2,1)}, u32[]{:S(2)}) copy-start(bf16[1024,512]{1,0:T(8,128)(2,1)} %param.14) | copy-start | bytes 3145732
  (3 other events, 2.2 us)
Sparse Core Ops, SparseCore 0:
  23.1 28.9 all-gather.2
  93.1 24.6 all-gather.4
  163.9 173.2 all-reduce.19
  339.4 84.3 reduce-scatter.2
  425.9 85.6 reduce-scatter.4
  515.1 88.0 all-reduce.17
